TPU v7x, 32 devices: a whole 2x2x4 slice. The times are simulated.
32 devices in a mesh: dp: 2 (over y), fsdp: 16 (over z, x, core).
Axes of the slice: x: 2, y: 2, z: 4, core: 2. Of those that a mesh axis runs over, the one named last changes fastest.
Arguments:
- ids: int32 [2, 192], P('dp'), may hold values from 0 to 511
- embed: bfloat16 [512, 8192], P(None, 'fsdp'), may hold values from -32 to 32
- gain: bfloat16 [8192], P('fsdp'), may hold values from 0.099609375 to 1.8984375
- w_in: bfloat16 [3, 4096, 8192], P(None, 'fsdp'), may hold values from -0.0625 to 0.0625
- feat_filter: float32 [3, 256, 7], P(None, 'fsdp'), may hold values from -2.4 to 2.4
- inner_filter: float32 [256, 7], P('fsdp'), may hold values from -2.4 to 2.4
- w_out: bfloat16 [4096, 8192], P(None, 'fsdp'), may hold values from -0.09375 to 0.09375
- cotangent: bfloat16 [2, 192, 8192], P('dp', None, 'fsdp'), may hold values from -6 to 6
- right_prev: bfloat16 [8192, 256], P('fsdp'), may hold values from -6 to 6
Outputs:
- block_out: bfloat16 [2, 192, 8192], P('dp', None, 'fsdp')
- filter_grad: float32 [4, 256, 7], P(None, 'fsdp')
- basis: bfloat16 [4096, 256], P('fsdp')
- right_factor: float32 [8192, 256], P('fsdp')
All inputs are finite; a program needn't handle non-finite values.
Results may differ from a plain program's by a relative error of at most 0.014.
The roundings to bfloat16 on the way count: a program that leaves them out, or rounds other values in their place, can miss the bound.
Values may be sent and summed in bfloat16 or wider, within the bound.
No kernel may reach another device: no remote copies, remote signals or barrier semaphores. Data moves between devices by JAX's collectives and lax.ppermute only.
A program may use at most 128 MiB of HBM per device.

v0:
```python
import jax
import jax.numpy as jnp
from jax import lax
from jax.sharding import PartitionSpec as P

D = 8192
C = 4096
GROUP = 16


def shifted(signal, lag, tap_count):
    padded = jnp.pad(signal, ((tap_count - 1, 0), (0, 0)))
    first = tap_count - 1 - lag
    return padded[first : first + signal.shape[0]]


def causal(signal, tap_table):
    tap_count = tap_table.shape[0]
    result = jnp.zeros(signal.shape, jnp.float32)
    for lag in range(tap_count):
        result = result + tap_table[lag][None, :] * shifted(signal, lag, tap_count)
    return result


def anticausal(signal, tap_table):
    tap_count = tap_table.shape[0]
    padded = jnp.pad(signal, ((0, tap_count - 1), (0, 0)))
    result = jnp.zeros(signal.shape, jnp.float32)
    for lag in range(tap_count):
        result = result + tap_table[lag][None, :] * padded[lag : lag + signal.shape[0]]
    return result


def tap_sums(gradient, signal, tap_count):
    listing = []
    for lag in range(tap_count):
        listing.append(jnp.sum(gradient * shifted(signal, lag, tap_count), axis=0))
    stacked = jnp.stack(listing, axis=0)
    grouped = stacked.reshape(tap_count, stacked.shape[1] // GROUP, GROUP).sum(axis=2)
    return grouped.T


def expand(filters):
    return jnp.repeat(filters.T, GROUP, axis=1)


def per_device(ids, embed, gain, w_in, feat_filter, inner_filter, w_out, cotangent, right_prev):
    tokens = ids[0]
    length = tokens.shape[0]
    tap_count = inner_filter.shape[1]
    onehot = (tokens[:, None] == jnp.arange(embed.shape[0], dtype=jnp.int32)[None, :]).astype(
        jnp.bfloat16
    )
    x_cols = jnp.dot(onehot, embed, preferred_element_type=jnp.float32)
    square_sums = lax.psum(jnp.sum(x_cols * x_cols, axis=1), "fsdp")
    factor = lax.rsqrt(square_sums / D + 1e-05)
    normed_cols = (x_cols * factor[:, None] * gain.astype(jnp.float32)[None, :]).astype(
        jnp.bfloat16
    )
    projected = jnp.einsum(
        "ld,kcd->klc",
        lax.all_gather(normed_cols, "fsdp", axis=1, tiled=True),
        w_in,
        preferred_element_type=jnp.float32,
    )
    rounded = lax.optimization_barrier(projected.astype(jnp.bfloat16)).astype(jnp.float32)
    query, key_in, value = (rounded[0], rounded[1], rounded[2])
    query_conv = causal(query, expand(feat_filter[0]))
    key_conv = causal(key_in, expand(feat_filter[1]))
    value_conv = causal(value, expand(feat_filter[2]))
    gated = key_conv * value_conv
    inner_table = expand(inner_filter)
    window = causal(gated, inner_table)
    gated_out = (query_conv * window).astype(jnp.bfloat16)
    cot_cols = cotangent[0]
    shard_piece = lax.all_gather(gated_out, "fsdp", axis=1, tiled=True)
    weight_rows = w_out
    mixed_sum = jnp.dot(shard_piece, weight_rows, preferred_element_type=jnp.float32)
    term = jnp.einsum("lc,ld->cd", shard_piece, cot_cols, preferred_element_type=jnp.float32)
    mixed_sum, grad_part = (mixed_sum, term)
    block_out = (x_cols + mixed_sum).astype(jnp.bfloat16)[None]
    weight_rows = w_out
    mixed_grad = lax.psum_scatter(
        jnp.einsum("cd,ld->cl", weight_rows, cot_cols, preferred_element_type=jnp.float32),
        "fsdp",
        scatter_dimension=0,
        tiled=True,
    ).T
    query_grad = mixed_grad * window
    window_grad = mixed_grad * query_conv
    gated_grad = anticausal(window_grad, inner_table)
    key_grad = gated_grad * value_conv
    value_grad = gated_grad * key_conv
    norm_factor = 1.0 / jnp.sqrt(jnp.float32(lax.axis_size("dp") * length))
    filter_part = (
        jnp.stack(
            [
                tap_sums(query_grad, query, tap_count),
                tap_sums(key_grad, key_in, tap_count),
                tap_sums(value_grad, value, tap_count),
                tap_sums(window_grad, gated, tap_count),
            ],
            axis=0,
        )
        * norm_factor
    )
    grad_total, filter_grad = (
        lax.psum(grad_part.astype(jnp.bfloat16), "dp").astype(jnp.float32),
        lax.psum(filter_part.astype(jnp.bfloat16), "dp").astype(jnp.float32),
    )
    grad_half = grad_total.astype(jnp.bfloat16)
    grad_rows_own = lax.all_to_all(grad_half, "fsdp", split_axis=0, concat_axis=1, tiled=True)
    panel_own = jnp.dot(
        grad_rows_own,
        lax.all_gather(right_prev, "fsdp", axis=0, tiled=True),
        preferred_element_type=jnp.float32,
    ).astype(jnp.bfloat16)
    root_scale = jnp.sqrt(jnp.float32(C))
    gram_local = jnp.einsum("cr,cs->rs", panel_own, panel_own, preferred_element_type=jnp.float32)
    gram_matrix = lax.psum(gram_local, "fsdp")
    lower_factor = jnp.linalg.cholesky(gram_matrix)
    solved = jax.scipy.linalg.solve_triangular(
        lower_factor, panel_own.astype(jnp.float32).T, lower=True
    ).T
    basis_own = (solved * root_scale).astype(jnp.bfloat16)
    right_raw = jnp.einsum(
        "cd,cr->dr",
        grad_half,
        lax.all_gather(basis_own, "fsdp", axis=0, tiled=True),
        preferred_element_type=jnp.float32,
    )
    column_sums = lax.psum(jnp.sum(right_raw * right_raw, axis=0), "fsdp")
    right_factor = right_raw * lax.rsqrt(column_sums / D + 1e-06)[None, :]
    return (block_out, filter_grad, basis_own, right_factor)


def solution(mesh):
    placed = (
        P("dp", None),
        P(None, "fsdp"),
        P("fsdp"),
        P(None, "fsdp", None),
        P(None, "fsdp", None),
        P("fsdp", None),
        P(None, "fsdp"),
        P("dp", None, "fsdp"),
        P("fsdp", None),
    )
    return jax.shard_map(
        per_device,
        mesh=mesh,
        in_specs=placed,
        out_specs=(P("dp", None, "fsdp"), P(None, "fsdp", None), P("fsdp", None), P("fsdp", None)),
        check_vma=False,
    )
```

profile of v0, /device:TPU:0, one launch (start us, length us, event | category | flops | bytes accessed | tf_op | source)
XLA Modules:
  0.0 699.4 jit_solution(17935779332028869934)
XLA Ops:
  9.3 34.9 %psum.35 = f32[192]{0:T(256)S(1)} all-reduce(f32[192]{0:T(256)S(1)} %get-tuple-element.121), channel_id=1, replica_groups=mesh['dp'=2,'fsdp'=16] {'fsdp'}, use_global_device_ids=true, to_apply=%region_1.0 | all-reduce | flops 192 | bytes 1536 | tf_op jit(solution)/shard_map/psum | solution.py:55
  45.1 5.4 fusion.14
  55.0 34.7 %all-gather.5.cloned.1.call-done = bf16[192,8192]{1,0:T(8,128)(2,1)} async-done(((bf16[192,512]{1,0:T(8,128)(2,1)}), bf16[192,8192]{1,0:T(8,128)(2,1)}) %all-gather.5.cloned.1.call-update) | async-done | bytes 3145744 | tf_op jit(solution)/shard_map/all_gather | solution.py:62
  89.7 9.8 %fusion.6 = bf16[3,192,256]{2,1,0:T(8,128)(2,1)S(1)} fusion(bf16[3,256,8192]{2,1,0:T(8,128)(2,1)} %param.12, bf16[192,8192]{1,0:T(8,128)(2,1)} %all-gather.5.cloned.1.call-done), kind=kOutput, calls=%fused_computation.8 | convolution fusion | flops 2416066560 | bytes 16023552 | tf_op jit(solution)/shard_map/ld,kcd->klc/dot_general | solution.py:60
  99.6 58.3 %reduce-scatter.2.cloned.1.call-done = f32[256,192]{0,1:T(8,128)} async-done(((f32[4096,192]{0,1:T(8,128)}), f32[256,192]{0,1:T(8,128)}) %reduce-scatter.2.cloned.1.call-update) | async-done | bytes 196624 | tf_op jit(solution)/shard_map/reduce_scatter | solution.py:83
  161.0 2.6 multiply_reduce_fusion.23
  164.3 38.0 %all-gather.7.cloned.1.call-done = bf16[192,4096]{1,0:T(8,128)(2,1)} async-done(((bf16[192,256]{1,0:T(8,128)(2,1)}), bf16[192,4096]{1,0:T(8,128)(2,1)}) %all-gather.7.cloned.1.call-update) | async-done | bytes 1572880 | tf_op jit(solution)/shard_map/all_gather | solution.py:76
  202.3 4.7 convolution_convert_fusion
  207.7 106.5 %all-reduce.9.cloned.1.call-done = bf16[4096,512]{1,0:T(8,128)(2,1)} async-done(((bf16[4096,512]{1,0:T(8,128)(2,1)}), bf16[4096,512]{1,0:T(8,128)(2,1)}) %all-reduce.9.cloned.1.call-update) | async-done | bytes 4194320 | tf_op jit(solution)/shard_map/psum | solution.py:108
  314.2 6.4 copy.22
  320.6 5.7 all-to-all-start
  326.3 94.7 %all-gather.9.cloned.1.call-done = bf16[8192,256]{1,0:T(8,128)(2,1)} async-done(((bf16[512,256]{1,0:T(8,128)(2,1)}), bf16[8192,256]{1,0:T(8,128)(2,1)}) %all-gather.9.cloned.1.call-update) | async-done | bytes 4194320 | tf_op jit(solution)/shard_map/all_gather | solution.py:115
  421.0 6.5 all-to-all-done
  427.4 4.8 convolution_convert_fusion.1
  434.0 103.0 %all-reduce.11.cloned.1.call-done = f32[256,256]{0,1:T(8,128)} async-done(((f32[256,256]{0,1:T(8,128)}), f32[256,256]{0,1:T(8,128)}) %all-reduce.11.cloned.1.call-update) | async-done | bytes 262160 | tf_op jit(solution)/shard_map/psum | solution.py:120
  537.0 1.8 copy.24
  540.6 11.7 %cholesky.50 = f32[128,128]{1,0:T(8,128)S(1)} custom-call(f32[128,128]{1,0:T(8,128)S(1)} %cholesky.118), custom_call_target="Cholesky" | custom-call | tf_op jit(solution)/shard_map/jit(cholesky)/cholesky | solution.py:121
  553.6 9.8 %custom-call.15 = f32[1,128,128]{1,2,0:T(8,128)S(1)} custom-call(f32[1,128,128]{2,1,0:T(8,128)S(1)} %get-tuple-element.89), custom_call_target="InvertDiagBlocksLowerTriangular" | custom-call | tf_op jit(solution)/shard_map/jit(cholesky)/cholesky | solution.py:121
  563.4 1.7 constant_dynamic-update-slice_fusion.29
  566.2 11.7 %cholesky.105 = f32[128,128]{1,0:T(8,128)S(1)} custom-call(f32[128,128]{1,0:T(8,128)S(1)} %convolution_subtract_fusion.1), custom_call_target="Cholesky" | custom-call | tf_op jit(solution)/shard_map/jit(cholesky)/cholesky | solution.py:121
  581.7 1.7 select_select_fusion
  584.2 6.8 while.1
  584.8 2.9 bitcast_dynamic-update-slice_fusion.2
  588.2 2.8 bitcast_dynamic-update-slice_fusion.2
  591.0 20.5 %custom-call.16 = f32[2,128,128]{1,2,0:T(8,128)S(1)} custom-call(f32[2,128,128]{2,1,0:T(8,128)} %get-tuple-element.11), custom_call_target="InvertDiagBlocksLowerTriangular" | custom-call | tf_op jit(solution)/shard_map/jit(_solve_triangular)/triangular_solve | solution.py:122
  614.0 1.9 multiply_reduce_fusion.2
  616.6 2.0 multiply_reduce_fusion.29
  622.1 5.0 psum.36
  627.8 3.8 fusion.9
  632.4 23.5 %all-gather.11.cloned.1.call-done = bf16[4096,256]{0,1:T(8,128)(2,1)} async-done(((bf16[256,256]{0,1:T(8,128)(2,1)}), bf16[4096,256]{0,1:T(8,128)(2,1)}) %all-gather.11.cloned.1.call-update) | async-done | bytes 2097168 | tf_op jit(solution)/shard_map/all_gather | solution.py:129
  655.9 4.2 multiply_reduce_fusion
  660.1 31.6 %psum.39 = f32[256]{0:T(256)S(1)} all-reduce(f32[256]{0:T(256)S(1)} %get-tuple-element.125), channel_id=1, replica_groups=mesh['dp'=2,'fsdp'=16] {'fsdp'}, use_global_device_ids=true, to_apply=%region_43.44 | all-reduce | flops 256 | bytes 2048 | tf_op jit(solution)/shard_map/psum | solution.py:132
  (190 shorter events, 31.1 us)
Async XLA Ops:
  7.2 1.1 copy-start
  7.2 82.5 %all-gather.5.cloned.1.call-start = ((), (), s32[]{:S(2)}) async-start(), calls=%async_computation.2 | async-start | bytes 3342336 | tf_op jit(solution)/shard_map/all_gather | solution.py:62
  45.0 5.5 copy-start.8
  45.0 6.6 copy-start.9
  45.1 112.9 %reduce-scatter.2.cloned.1.call-start = ((), (), s32[]{:S(2)}) async-start(), calls=%async_computation.4 | async-start | bytes 3342336 | tf_op jit(solution)/shard_map/reduce_scatter | solution.py:83
  50.5 151.8 %all-gather.7.cloned.1.call-start = ((), (), s32[]{:S(2)}) async-start(), calls=%async_computation.3 | async-start | bytes 1671168 | tf_op jit(solution)/shard_map/all_gather | solution.py:76
  99.5 102.8 %copy-start.7 = (bf16[1,192,512]{2,1,0:T(8,128)(2,1)S(1)}, bf16[1,192,512]{2,1,0:T(8,128)(2,1)}, u32[]{:S(2)}) copy-start(bf16[1,192,512]{2,1,0:T(8,128)(2,1)} %param.16) | copy-start | bytes 589828
  99.6 61.3 %copy-start.3 = (f32[192,256]{1,0:T(8,128)}, f32[192,256]{1,0:T(8,128)S(1)}, u32[]{:S(2)}) copy-start(f32[192,256]{1,0:T(8,128)S(1)} %get-tuple-element.84) | copy-start | bytes 589828
  159.1 48.0 %copy-start.4 = (f32[192,256]{1,0:T(8,128)}, f32[192,256]{1,0:T(8,128)S(1)}, u32[]{:S(2)}) copy-start(f32[192,256]{1,0:T(8,128)S(1)} %get-tuple-element.79) | copy-start | bytes 589828
  161.0 46.1 %copy-start.2 = (f32[192,256]{1,0:T(8,128)}, f32[192,256]{1,0:T(8,128)S(1)}, u32[]{:S(2)}) copy-start(f32[192,256]{1,0:T(8,128)S(1)} %mul.459) | copy-start | bytes 589828
  164.2 150.0 %all-reduce.9.cloned.1.call-start = ((), (), s32[]{:S(2)}) async-start(), calls=%async_computation.5 | async-start | bytes 8388608 | tf_op jit(solution)/shard_map/psum | solution.py:108
  207.1 213.9 %all-gather.9.cloned.1.call-start = ((), (), s32[]{:S(2)}) async-start(), calls=%async_computation.6 | async-start | bytes 4456448 | tf_op jit(solution)/shard_map/all_gather | solution.py:115
  320.6 106.8 %all-to-all-start = ((bf16[16,256,512]{1,2,0:T(8,128)(2,1)}), bf16[16,256,512]{1,2,0:T(8,128)(2,1)}, u32[]{:S(2)}, u32[]{:S(2)}) async-start(bf16[16,256,512]{1,2,0:T(8,128)(2,1)} %copy.22), calls=%async_computation.1 | async-start | bytes 8388608 | tf_op jit(solution)/shard_map/all_to_all | solution.py:112
  326.2 210.8 %all-reduce.11.cloned.1.call-start = ((), (), s32[]{:S(2)}) async-start(), calls=%async_computation.7 | async-start | bytes 524288 | tf_op jit(solution)/shard_map/psum | solution.py:120
  433.2 222.7 %all-gather.11.cloned.1.call-start = ((), (), s32[]{:S(2)}) async-start(), calls=%async_computation.8 | async-start | bytes 2228224 | tf_op jit(solution)/shard_map/all_gather | solution.py:129
  434.0 193.8 %copy-start.1 = (bf16[192,4096]{1,0:T(8,128)(2,1)S(1)}, bf16[192,4096]{1,0:T(8,128)(2,1)}, u32[]{:S(2)}) copy-start(bf16[192,4096]{1,0:T(8,128)(2,1)} %all-gather.7.cloned.1.call-done) | copy-start | bytes 4718596
  539.9 0.7 copy-start.6
  616.6 15.0 %copy-start.5 = (bf16[256,256]{0,1:T(8,128)(2,1)S(1)}, bf16[256,256]{0,1:T(8,128)(2,1)}, u32[]{:S(2)}) copy-start(bf16[256,256]{0,1:T(8,128)(2,1)} %fusion.19) | copy-start | bytes 393220
Sparse Core Ops, SparseCore 0:
  45.2 44.4 all-gather.4
  93.5 64.4 reduce-scatter.1
  164.4 37.9 all-gather.6
  207.2 106.9 all-reduce.8
  316.4 104.4 all-gather.8
  433.3 103.7 all-reduce.10
  614.1 41.7 all-gather.10
where the time goes:
time: 700 us; the launch traced here: 699 us
  waiting for transfers between devices  466 us (67%)
  other arithmetic  73.8 us (11%)
  blocking collectives  71.5 us (10%)
  matrix products  39.3 us (6%)
  local copies, waits for them, and re-layouts  26.9 us (4%)
  between operations  15.8 us (2%)
    psum x1, waiting for transfers between devices, per_device(): lax.psum(grad_part.astype(jnp.bfloat16), 'dp').astype(jnp.float32)  107 us
    psum x1, waiting for transfers between devices, per_device(): gram_matrix = lax.psum(gram_local, 'fsdp')  103 us
    all_gather x1, waiting for transfers between devices, per_device(): lax.all_gather(right_prev, 'fsdp', axis=0, tiled=True)  94.7 us
    reduce_scatter x1, waiting for transfers between devices, per_device(): lax.psum_scatter(jnp.einsum('cd,ld->cl', weight_rows, cot_cols, preferred...  58.3 us
    all_gather x1, waiting for transfers between devices, per_device(): shard_piece = lax.all_gather(gated_out, 'fsdp', axis=1, tiled=True)  38 us
    another operation x7, other arithmetic, per_device(): lower_factor = jnp.linalg.cholesky(gram_matrix)  36.4 us
    psum x1, blocking collectives, per_device(): square_sums = lax.psum(jnp.sum(x_cols * x_cols, axis=1), 'fsdp')  34.9 us
    all_gather x1, waiting for transfers between devices, per_device(): lax.all_gather(normed_cols, 'fsdp', axis=1, tiled=True)  34.7 us
  transfers between devices with their start and end apart: 8, of which 8 were waited for; matrix products, arithmetic and copies ran while one was open for 6% of the time, Pallas kernels for 0%

commit v1 on v0

--- a/solution.py
+++ b/solution.py
@@ -6,6 +6,22 @@
 D = 8192
 C = 4096
 GROUP = 16
+
+
+def summed_both_ways(x, axis, dim, term):
+    size, place, width = (lax.axis_size(axis), lax.axis_index(axis), x.shape[dim])
+    forward = [(i, (i + 1) % size) for i in range(size)]
+    left = [(i, (i - 1) % size) for i in range(size)]
+    half = size // 2
+    from_left = from_right = x
+    running = term(x, place * width)
+    for step in range(1, half + 1):
+        from_left = lax.ppermute(from_left, axis, forward)
+        if step < size - half:
+            from_right = lax.ppermute(from_right, axis, left)
+            running = running + term(from_right, (place + step) % size * width)
+        running = running + term(from_left, (place - step) % size * width)
+    return running
 
 
 def shifted(signal, lag, tap_count):
@@ -123,11 +139,16 @@
         lower_factor, panel_own.astype(jnp.float32).T, lower=True
     ).T
     basis_own = (solved * root_scale).astype(jnp.bfloat16)
-    right_raw = jnp.einsum(
-        "cd,cr->dr",
-        grad_half,
-        lax.all_gather(basis_own, "fsdp", axis=0, tiled=True),
-        preferred_element_type=jnp.float32,
+    right_raw = summed_both_ways(
+        basis_own,
+        "fsdp",
+        0,
+        lambda shard, start: jnp.einsum(
+            "cd,cr->dr",
+            lax.dynamic_slice_in_dim(grad_half, start, shard.shape[0], axis=0),
+            shard,
+            preferred_element_type=jnp.float32,
+        ),
     )
     column_sums = lax.psum(jnp.sum(right_raw * right_raw, axis=0), "fsdp")
     right_factor = right_raw * lax.rsqrt(column_sums / D + 1e-06)[None, :]

time: 700 us -> 699 us (level)
  starting transfers between devices: 6.13 us -> 38.1 us
  waiting for transfers between devices: 466 us -> 449 us
  other arithmetic: 73.8 us -> 63.1 us
    ppermute x0 -> x15, starting transfers between devices: none -> 32.2 us  [the longest x7 31.5 us: summed_both_ways(): from_right = lax.ppermute(from_right, axis, left)]
    all_gather x1 -> x0, waiting for transfers between devices: 23.5 us -> none  [per_device(): lax.all_gather(basis_own, 'fsdp', axis=0, tiled=True)]
    ppermute x0 -> x15, waiting for transfers between devices: none -> 15.7 us  [the longest x8 11.7 us: summed_both_ways(): from_left = lax.ppermute(from_left, axis, forward)]
  transfers between devices with their start and end apart: 8 -> 22, of which waited for: 8 -> 19; matrix products, arithmetic and copies ran while one was open for 6% -> 6% of each run, Pallas kernels for 0% -> 0%
where the time goes in v1:
time: 699 us; the launch traced here: 698 us
  waiting for transfers between devices  449 us (64%)
  blocking collectives  69.4 us (10%)
  other arithmetic  63.1 us (9%)
  matrix products  40.3 us (6%)
  starting transfers between devices  38.1 us (5%)
  local copies, waits for them, and re-layouts  21 us (3%)
  between operations  16.4 us (2%)
    psum x1, waiting for transfers between devices, per_device(): lax.psum(grad_part.astype(jnp.bfloat16), 'dp').astype(jnp.float32)  107 us
    psum x1, waiting for transfers between devices, per_device(): gram_matrix = lax.psum(gram_local, 'fsdp')  97.8 us
    all_gather x1, waiting for transfers between devices, per_device(): lax.all_gather(right_prev, 'fsdp', axis=0, tiled=True)  91.2 us
    reduce_scatter x1, waiting for transfers between devices, per_device(): lax.psum_scatter(jnp.einsum('cd,ld->cl', weight_rows, cot_cols, preferred...  58.4 us
    all_gather x1, waiting for transfers between devices, per_device(): shard_piece = lax.all_gather(gated_out, 'fsdp', axis=1, tiled=True)  38.1 us
    psum x1, blocking collectives, per_device(): square_sums = lax.psum(jnp.sum(x_cols * x_cols, axis=1), 'fsdp')  34.9 us
    all_gather x1, waiting for transfers between devices, per_device(): lax.all_gather(normed_cols, 'fsdp', axis=1, tiled=True)  34.7 us
    another operation x7, other arithmetic, per_device(): lower_factor = jnp.linalg.cholesky(gram_matrix)  34.6 us
  transfers between devices with their start and end apart: 22, of which 19 were waited for; matrix products, arithmetic and copies ran while one was open for 6% of the time, Pallas kernels for 0%

profile of v1, /device:TPU:0, one launch (start us, length us, event | category | flops | bytes accessed | tf_op | source)
XLA Modules:
  0.0 697.9 jit_solution(12297528225318314122)
XLA Ops:
  9.3 34.9 %psum.35 = f32[192]{0:T(256)S(1)} all-reduce(f32[192]{0:T(256)S(1)} %get-tuple-element.121), channel_id=1, replica_groups=mesh['dp'=2,'fsdp'=16] {'fsdp'}, use_global_device_ids=true, to_apply=%region_1.0 | all-reduce | flops 192 | bytes 1536 | tf_op jit(solution)/shard_map/psum | solution.py:71
  45.1 5.4 fusion.43
  55.0 34.7 %all-gather.4.cloned.1.call-done = bf16[192,8192]{1,0:T(8,128)(2,1)} async-done(((bf16[192,512]{1,0:T(8,128)(2,1)}), bf16[192,8192]{1,0:T(8,128)(2,1)}) %all-gather.4.cloned.1.call-update) | async-done | bytes 3145744 | tf_op jit(solution)/shard_map/all_gather | solution.py:78
  89.7 9.8 %fusion.12 = bf16[3,192,256]{2,1,0:T(8,128)(2,1)S(1)} fusion(bf16[3,256,8192]{2,1,0:T(8,128)(2,1)} %param.12, bf16[192,8192]{1,0:T(8,128)(2,1)} %all-gather.4.cloned.1.call-done), kind=kOutput, calls=%fused_computation.23 | convolution fusion | flops 2416066560 | bytes 16023552 | tf_op jit(solution)/shard_map/ld,kcd->klc/dot_general | solution.py:76
  99.6 58.4 %reduce-scatter.2.cloned.1.call-done = f32[256,192]{0,1:T(8,128)} async-done(((f32[4096,192]{0,1:T(8,128)}), f32[256,192]{0,1:T(8,128)}) %reduce-scatter.2.cloned.1.call-update) | async-done | bytes 196624 | tf_op jit(solution)/shard_map/reduce_scatter | solution.py:99
  161.6 38.1 %all-gather.6.cloned.1.call-done = bf16[192,4096]{1,0:T(8,128)(2,1)} async-done(((bf16[192,256]{1,0:T(8,128)(2,1)}), bf16[192,4096]{1,0:T(8,128)(2,1)}) %all-gather.6.cloned.1.call-update) | async-done | bytes 1572880 | tf_op jit(solution)/shard_map/all_gather | solution.py:92
  199.7 4.7 convolution_convert_fusion
  205.0 106.5 %all-reduce.9.cloned.1.call-done = bf16[4096,512]{1,0:T(8,128)(2,1)} async-done(((bf16[4096,512]{1,0:T(8,128)(2,1)}), bf16[4096,512]{1,0:T(8,128)(2,1)}) %all-reduce.9.cloned.1.call-update) | async-done | bytes 4194320 | tf_op jit(solution)/shard_map/psum | solution.py:124
  311.6 6.4 copy.22
  317.9 5.7 all-to-all-start
  327.1 91.2 %all-gather.8.cloned.1.call-done = bf16[8192,256]{1,0:T(8,128)(2,1)} async-done(((bf16[512,256]{1,0:T(8,128)(2,1)}), bf16[8192,256]{1,0:T(8,128)(2,1)}) %all-gather.8.cloned.1.call-update) | async-done | bytes 4194320 | tf_op jit(solution)/shard_map/all_gather | solution.py:131
  418.3 6.5 all-to-all-done
  424.8 4.8 convolution_convert_fusion.1
  430.9 5.0 psum.36
  436.5 97.8 %all-reduce.11.cloned.1.call-done = f32[256,256]{0,1:T(8,128)} async-done(((f32[256,256]{0,1:T(8,128)}), f32[256,256]{0,1:T(8,128)}) %all-reduce.11.cloned.1.call-update) | async-done | bytes 262160 | tf_op jit(solution)/shard_map/psum | solution.py:136
  536.5 11.7 %cholesky.50 = f32[128,128]{1,0:T(8,128)S(1)} custom-call(f32[128,128]{1,0:T(8,128)S(1)} %cholesky.118), custom_call_target="Cholesky" | custom-call | tf_op jit(solution)/shard_map/jit(cholesky)/cholesky | solution.py:137
  548.3 9.8 %custom-call.15 = f32[1,128,128]{1,2,0:T(8,128)S(1)} custom-call(f32[1,128,128]{2,1,0:T(8,128)S(1)} %get-tuple-element.89), custom_call_target="InvertDiagBlocksLowerTriangular" | custom-call | tf_op jit(solution)/shard_map/jit(cholesky)/cholesky | solution.py:137
  558.5 11.7 %cholesky.105 = f32[128,128]{1,0:T(8,128)S(1)} custom-call(f32[128,128]{1,0:T(8,128)S(1)} %convolution_subtract_fusion.1), custom_call_target="Cholesky" | custom-call | tf_op jit(solution)/shard_map/jit(cholesky)/cholesky | solution.py:137
  573.0 5.3 while.1
  573.7 2.0 bitcast_dynamic-update-slice_fusion.2
  576.3 2.0 bitcast_dynamic-update-slice_fusion.2
  578.3 20.5 %custom-call.16 = f32[2,128,128]{1,2,0:T(8,128)S(1)} custom-call(f32[2,128,128]{2,1,0:T(8,128)} %get-tuple-element.11), custom_call_target="InvertDiagBlocksLowerTriangular" | custom-call | tf_op jit(solution)/shard_map/jit(_solve_triangular)/triangular_solve | solution.py:138
  600.4 3.9 collective-permute-start
  604.3 3.9 fusion.15
  610.4 4.4 collective-permute-start.2
  618.7 4.5 collective-permute-start.4
  625.7 4.7 collective-permute-start.6
  632.9 4.7 collective-permute-start.8
  640.1 4.7 collective-permute-start.10
  647.3 4.7 collective-permute-start.12
  654.7 5.7 collective-permute-done.14
  660.7 29.5 %psum.39 = f32[256]{0:T(256)S(1)} all-reduce(f32[256]{0:T(256)S(1)} %get-tuple-element.125), channel_id=1, replica_groups=mesh['dp'=2,'fsdp'=16] {'fsdp'}, use_global_device_ids=true, to_apply=%region_43.44 | all-reduce | flops 256 | bytes 2048 | tf_op jit(solution)/shard_map/psum | solution.py:153
  (224 shorter events, 43.3 us)
Async XLA Ops:
  7.2 1.1 copy-start
  7.2 82.5 %all-gather.4.cloned.1.call-start = ((), (), s32[]{:S(2)}) async-start(), calls=%async_computation.2 | async-start | bytes 3342336 | tf_op jit(solution)/shard_map/all_gather | solution.py:78
  45.0 5.6 copy-start.4
  45.0 6.6 copy-start.5
  45.1 112.9 %reduce-scatter.2.cloned.1.call-start = ((), (), s32[]{:S(2)}) async-start(), calls=%async_computation.4 | async-start | bytes 3342336 | tf_op jit(solution)/shard_map/reduce_scatter | solution.py:99
  50.5 149.2 %all-gather.6.cloned.1.call-start = ((), (), s32[]{:S(2)}) async-start(), calls=%async_computation.3 | async-start | bytes 1671168 | tf_op jit(solution)/shard_map/all_gather | solution.py:92
  99.5 100.2 %copy-start.3 = (bf16[1,192,512]{2,1,0:T(8,128)(2,1)S(1)}, bf16[1,192,512]{2,1,0:T(8,128)(2,1)}, u32[]{:S(2)}) copy-start(bf16[1,192,512]{2,1,0:T(8,128)(2,1)} %param.16) | copy-start | bytes 589828
  161.6 150.0 %all-reduce.9.cloned.1.call-start = ((), (), s32[]{:S(2)}) async-start(), calls=%async_computation.5 | async-start | bytes 8388608 | tf_op jit(solution)/shard_map/psum | solution.py:124
  204.4 213.9 %all-gather.8.cloned.1.call-start = ((), (), s32[]{:S(2)}) async-start(), calls=%async_computation.6 | async-start | bytes 4456448 | tf_op jit(solution)/shard_map/all_gather | solution.py:131
  317.9 106.8 %all-to-all-start = ((bf16[16,256,512]{1,2,0:T(8,128)(2,1)}), bf16[16,256,512]{1,2,0:T(8,128)(2,1)}, u32[]{:S(2)}, u32[]{:S(2)}) async-start(bf16[16,256,512]{1,2,0:T(8,128)(2,1)} %copy.22), calls=%async_computation.1 | async-start | bytes 8388608 | tf_op jit(solution)/shard_map/all_to_all | solution.py:128
  323.6 210.8 %all-reduce.11.cloned.1.call-start = ((), (), s32[]{:S(2)}) async-start(), calls=%async_computation.7 | async-start | bytes 524288 | tf_op jit(solution)/shard_map/psum | solution.py:136
  429.6 174.7 %copy-start.2 = (bf16[192,4096]{1,0:T(8,128)(2,1)S(1)}, bf16[192,4096]{1,0:T(8,128)(2,1)}, u32[]{:S(2)}) copy-start(bf16[192,4096]{1,0:T(8,128)(2,1)} %all-gather.6.cloned.1.call-done) | copy-start | bytes 4718596
  599.8 10.5 %collective-permute-start.1 = (bf16[256,256]{0,1:T(8,128)(2,1)S(1)}, bf16[256,256]{0,1:T(8,128)(2,1)S(1)}, u32[]{:S(2)}, u32[]{:S(2)}) collective-permute-start(bf16[256,256]{0,1:T(8,128)(2,1)S(1)} %fusion.73), channel_id=1, source_target_pairs={{0,1},{1,2},{2,3},{3,4},{4,5},{5,6},{6,7},{7,8},{8,9},{9,10},{10,1... | collective-permute-start | bytes 393224 | tf_op jit(solution)/shard_map/ppermute | solution.py:19
  600.4 10.0 %collective-permute-start = (bf16[256,256]{0,1:T(8,128)(2,1)S(1)}, bf16[256,256]{0,1:T(8,128)(2,1)S(1)}, u32[]{:S(2)}, u32[]{:S(2)}) collective-permute-start(bf16[256,256]{0,1:T(8,128)(2,1)S(1)} %fusion.73), channel_id=1, source_target_pairs={{0,15},{1,0},{2,1},{3,2},{4,3},{5,4},{6,5},{7,6},{8,7},{9,8},{10,9... | collective-permute-start | bytes 393224 | tf_op jit(solution)/shard_map/ppermute | solution.py:21
  608.9 14.2 %copy-start.1 = (bf16[4096,512]{1,0:T(8,128)(2,1)S(1)}, bf16[4096,512]{1,0:T(8,128)(2,1)}, u32[]{:S(2)}) copy-start(bf16[4096,512]{1,0:T(8,128)(2,1)} %all-reduce.9.cloned.1.call-done) | copy-start | bytes 12582916
  610.3 7.1 %collective-permute-start.3 = (bf16[256,256]{0,1:T(8,128)(2,1)S(1)}, bf16[256,256]{0,1:T(8,128)(2,1)S(1)}, u32[]{:S(2)}, u32[]{:S(2)}) collective-permute-start(bf16[256,256]{0,1:T(8,128)(2,1)S(1)} %collective-permute-done.1), channel_id=1, source_target_pairs={{0,1},{1,2},{2,3},{3,4},{4,5},{5,6},{6,7},{7,8},{8,9},{9,10},{10,1... | collective-permute-start | bytes 393224 | tf_op jit(solution)/shard_map/ppermute | solution.py:19
  610.4 8.3 %collective-permute-start.2 = (bf16[256,256]{0,1:T(8,128)(2,1)S(1)}, bf16[256,256]{0,1:T(8,128)(2,1)S(1)}, u32[]{:S(2)}, u32[]{:S(2)}) collective-permute-start(bf16[256,256]{0,1:T(8,128)(2,1)S(1)} %collective-permute-done), channel_id=1, source_target_pairs={{0,15},{1,0},{2,1},{3,2},{4,3},{5,4},{6,5},{7,6},{8,7},{9,8},{10,9... | collective-permute-start | bytes 393224 | tf_op jit(solution)/shard_map/ppermute | solution.py:21
  617.4 7.2 %collective-permute-start.5 = (bf16[256,256]{0,1:T(8,128)(2,1)S(1)}, bf16[256,256]{0,1:T(8,128)(2,1)S(1)}, u32[]{:S(2)}, u32[]{:S(2)}) collective-permute-start(bf16[256,256]{0,1:T(8,128)(2,1)S(1)} %collective-permute-done.3), channel_id=1, source_target_pairs={{0,1},{1,2},{2,3},{3,4},{4,5},{5,6},{6,7},{7,8},{8,9},{9,10},{10,1... | collective-permute-start | bytes 393224 | tf_op jit(solution)/shard_map/ppermute | solution.py:19
  618.7 7.0 %collective-permute-start.4 = (bf16[256,256]{0,1:T(8,128)(2,1)S(1)}, bf16[256,256]{0,1:T(8,128)(2,1)S(1)}, u32[]{:S(2)}, u32[]{:S(2)}) collective-permute-start(bf16[256,256]{0,1:T(8,128)(2,1)S(1)} %collective-permute-done.2), channel_id=1, source_target_pairs={{0,15},{1,0},{2,1},{3,2},{4,3},{5,4},{6,5},{7,6},{8,7},{9,8},{10,9... | collective-permute-start | bytes 393224 | tf_op jit(solution)/shard_map/ppermute | solution.py:21
  624.6 7.2 %collective-permute-start.7 = (bf16[256,256]{0,1:T(8,128)(2,1)S(1)}, bf16[256,256]{0,1:T(8,128)(2,1)S(1)}, u32[]{:S(2)}, u32[]{:S(2)}) collective-permute-start(bf16[256,256]{0,1:T(8,128)(2,1)S(1)} %collective-permute-done.5), channel_id=1, source_target_pairs={{0,1},{1,2},{2,3},{3,4},{4,5},{5,6},{6,7},{7,8},{8,9},{9,10},{10,1... | collective-permute-start | bytes 393224 | tf_op jit(solution)/shard_map/ppermute | solution.py:19
  625.7 7.2 %collective-permute-start.6 = (bf16[256,256]{0,1:T(8,128)(2,1)S(1)}, bf16[256,256]{0,1:T(8,128)(2,1)S(1)}, u32[]{:S(2)}, u32[]{:S(2)}) collective-permute-start(bf16[256,256]{0,1:T(8,128)(2,1)S(1)} %collective-permute-done.4), channel_id=1, source_target_pairs={{0,15},{1,0},{2,1},{3,2},{4,3},{5,4},{6,5},{7,6},{8,7},{9,8},{10,9... | collective-permute-start | bytes 393224 | tf_op jit(solution)/shard_map/ppermute | solution.py:21
  631.8 7.2 %collective-permute-start.9 = (bf16[256,256]{0,1:T(8,128)(2,1)S(1)}, bf16[256,256]{0,1:T(8,128)(2,1)S(1)}, u32[]{:S(2)}, u32[]{:S(2)}) collective-permute-start(bf16[256,256]{0,1:T(8,128)(2,1)S(1)} %collective-permute-done.7), channel_id=1, source_target_pairs={{0,1},{1,2},{2,3},{3,4},{4,5},{5,6},{6,7},{7,8},{8,9},{9,10},{10,1... | collective-permute-start | bytes 393224 | tf_op jit(solution)/shard_map/ppermute | solution.py:19
  632.9 7.2 %collective-permute-start.8 = (bf16[256,256]{0,1:T(8,128)(2,1)S(1)}, bf16[256,256]{0,1:T(8,128)(2,1)S(1)}, u32[]{:S(2)}, u32[]{:S(2)}) collective-permute-start(bf16[256,256]{0,1:T(8,128)(2,1)S(1)} %collective-permute-done.6), channel_id=1, source_target_pairs={{0,15},{1,0},{2,1},{3,2},{4,3},{5,4},{6,5},{7,6},{8,7},{9,8},{10,9... | collective-permute-start | bytes 393224 | tf_op jit(solution)/shard_map/ppermute | solution.py:21
  639.0 7.2 %collective-permute-start.11 = (bf16[256,256]{0,1:T(8,128)(2,1)S(1)}, bf16[256,256]{0,1:T(8,128)(2,1)S(1)}, u32[]{:S(2)}, u32[]{:S(2)}) collective-permute-start(bf16[256,256]{0,1:T(8,128)(2,1)S(1)} %collective-permute-done.9), channel_id=1, source_target_pairs={{0,1},{1,2},{2,3},{3,4},{4,5},{5,6},{6,7},{7,8},{8,9},{9,10},{10,1... | collective-permute-start | bytes 393224 | tf_op jit(solution)/shard_map/ppermute | solution.py:19
  640.1 7.2 %collective-permute-start.10 = (bf16[256,256]{0,1:T(8,128)(2,1)S(1)}, bf16[256,256]{0,1:T(8,128)(2,1)S(1)}, u32[]{:S(2)}, u32[]{:S(2)}) collective-permute-start(bf16[256,256]{0,1:T(8,128)(2,1)S(1)} %collective-permute-done.8), channel_id=1, source_target_pairs={{0,15},{1,0},{2,1},{3,2},{4,3},{5,4},{6,5},{7,6},{8,7},{9,8},{10,9... | collective-permute-start | bytes 393224 | tf_op jit(solution)/shard_map/ppermute | solution.py:21
  646.2 7.1 %collective-permute-start.13 = (bf16[256,256]{0,1:T(8,128)(2,1)S(1)}, bf16[256,256]{0,1:T(8,128)(2,1)S(1)}, u32[]{:S(2)}, u32[]{:S(2)}) collective-permute-start(bf16[256,256]{0,1:T(8,128)(2,1)S(1)} %collective-permute-done.11), channel_id=1, source_target_pairs={{0,1},{1,2},{2,3},{3,4},{4,5},{5,6},{6,7},{7,8},{8,9},{9,10},{10,1... | collective-permute-start | bytes 393224 | tf_op jit(solution)/shard_map/ppermute | solution.py:19
  647.3 7.2 %collective-permute-start.12 = (bf16[256,256]{0,1:T(8,128)(2,1)S(1)}, bf16[256,256]{0,1:T(8,128)(2,1)S(1)}, u32[]{:S(2)}, u32[]{:S(2)}) collective-permute-start(bf16[256,256]{0,1:T(8,128)(2,1)S(1)} %collective-permute-done.10), channel_id=1, source_target_pairs={{0,15},{1,0},{2,1},{3,2},{4,3},{5,4},{6,5},{7,6},{8,7},{9,8},{10,9... | collective-permute-start | bytes 393224 | tf_op jit(solution)/shard_map/ppermute | solution.py:21
  653.3 7.1 %collective-permute-start.14 = (bf16[256,256]{0,1:T(8,128)(2,1)S(1)}, bf16[256,256]{0,1:T(8,128)(2,1)S(1)}, u32[]{:S(2)}, u32[]{:S(2)}) collective-permute-start(bf16[256,256]{0,1:T(8,128)(2,1)S(1)} %collective-permute-done.13), channel_id=1, source_target_pairs={{0,1},{1,2},{2,3},{3,4},{4,5},{5,6},{6,7},{7,8},{8,9},{9,10},{10,1... | collective-permute-start | bytes 393224 | tf_op jit(solution)/shard_map/ppermute | solution.py:19
Sparse Core Ops, SparseCore 0:
  45.2 44.4 all-gather.3
  93.5 64.4 reduce-scatter.1
  161.7 37.9 all-gather.5
  204.5 106.9 all-reduce.8
  313.8 104.4 all-gather.7
  430.6 103.7 all-reduce.10
